TPU v7x, 256 devices: a whole 4x4x8 slice. The times are simulated.
256 devices in a mesh: pole: 8 (over y, x_lo), leaf: 32 (over x_hi, z, core).
Axes of the slice: x: 4 (x_hi: 2, x_lo: 2; x = x_hi * 2 + x_lo), y: 4, z: 8, core: 2. Of those that a mesh axis runs over, the one named last changes fastest.
Arguments:
- inverse_front: bfloat16 [8, 2, 8192, 8192], P('pole', None, 'leaf'), may hold values from -6 to 6
- factor_panel: bfloat16 [8, 8192, 512], P('pole', 'leaf'), may hold values from -0.0625 to 0.0625
- diag_inverse: bfloat16 [8, 256, 512], P('pole'), may hold values from -6 to 6
- pole_weight: float32 [8, 2], P('pole'), may hold values from -2.4 to 2.4
- structure: int32 [32], replicated, may hold values from 0 to 1, as said below
- block_owner: int32 [1024, 1], P('leaf'), may hold values from 0 to 31; in each aligned block of 32 rows (0 to 31, 32 to 63, ...) at most 2 rows name the same one
Outputs:
- owned_density: float32 [2048, 8, 256], P('leaf')
- diag_density: float32 [256, 256], replicated
Inputs may be any that keep to these rules, and one draw needn't show every extreme that they name: `structure`: exactly 16 entries are 1. `block_owner`: among the 32 blocks of one index of leaf no owner appears more than 2 times, and in some index's blocks one owner appears exactly 2 times.
All inputs are finite; a program needn't handle non-finite values.
Results may differ from a plain program's by a relative error of at most 0.0003.
Values may be sent and summed in bfloat16 or wider, within the bound.
No kernel may reach another device: no remote copies, remote signals or barrier semaphores. Data moves between devices by JAX's collectives and lax.ppermute only.
A program may use at most 64 MiB of HBM per device.

v0:
```python
import jax
import jax.numpy as jnp
from jax import lax
from jax.sharding import PartitionSpec as P


def kept_rows(structure, first_row, row_count, block_width):
    block_ids = jnp.arange(structure.shape[0], dtype=jnp.int32)
    which_block = (first_row + jnp.arange(row_count, dtype=jnp.int32)) // block_width
    matches = which_block[:, None] == block_ids[None, :]
    return jnp.sum(jnp.where(matches, structure[None, :], 0), axis=1).astype(jnp.float32)


def panel_product(columns, panel):
    return jnp.einsum("pcrk,pkn->pcrn", columns, panel, preferred_element_type=jnp.float32)


def body(inverse_front, factor_panel, diag_inverse, pole_weight, structure, block_owner):
    leaves = lax.axis_size("leaf")
    rows_here = inverse_front.shape[2]
    block_width = factor_panel.shape[2] // 2
    first_row = lax.axis_index("leaf") * rows_here
    panel_rows = lax.all_gather(factor_panel, "leaf", axis=1, tiled=True)
    row_count = panel_rows.shape[1]
    keep_piece = kept_rows(structure, jnp.int32(0), row_count, block_width).astype(jnp.bfloat16)
    masked = panel_rows * keep_piece[None, :, None]
    product = panel_product(inverse_front, masked)
    keep_here = kept_rows(structure, first_row, rows_here, block_width)[None, :, None]
    block_real = -(product[:, 0, :, :block_width] - product[:, 1, :, block_width:]) * keep_here
    block_imag = -(product[:, 0, :, block_width:] + product[:, 1, :, :block_width]) * keep_here
    weight_real = pole_weight[:, 0][:, None, None]
    weight_imag = pole_weight[:, 1][:, None, None]
    density_part = jnp.sum(weight_real * block_imag + weight_imag * block_real, axis=0)
    panel_kept = factor_panel.astype(jnp.float32) * keep_here
    panel_real = panel_kept[:, :, :block_width]
    panel_imag = panel_kept[:, :, block_width:]
    precise = lax.Precision.HIGHEST

    def transposed(left_side, right_side):
        return jnp.einsum("prk,prn->pkn", left_side, right_side, precision=precise)

    schur_real = transposed(panel_real, block_real) - transposed(panel_imag, block_imag)
    schur_imag = transposed(panel_real, block_imag) + transposed(panel_imag, block_real)
    diag_full = diag_inverse.astype(jnp.float32)
    schur_real, schur_imag = lax.psum((schur_real, schur_imag), "leaf")
    corner_real = diag_full[:, :, :block_width] - schur_real
    corner_imag = diag_full[:, :, block_width:] - schur_imag
    corner_terms = jnp.sum(weight_real * corner_imag + weight_imag * corner_real, axis=0)
    diag_density = lax.psum(corner_terms, "pole")
    blocks_mine = block_owner.shape[0]
    element_rows = rows_here // blocks_mine
    capacity = max(2, (2 * blocks_mine + leaves - 1) // leaves)
    owners = block_owner[:, 0]
    one_hot = (owners[:, None] == jnp.arange(leaves, dtype=jnp.int32)[None, :]).astype(jnp.int32)
    ranks = jnp.sum((jnp.cumsum(one_hot, axis=0) - one_hot) * one_hot, axis=1)
    slot_index = owners * capacity + ranks
    density_rows = lax.psum(density_part, "pole")
    column_count = density_rows.shape[1]
    element_blocks = density_rows.reshape(blocks_mine, element_rows, column_count)
    buffer_zero = jnp.zeros((leaves * capacity, element_rows, column_count), jnp.float32)
    owned_density = lax.all_to_all(
        buffer_zero.at[slot_index].set(element_blocks),
        "leaf",
        split_axis=0,
        concat_axis=0,
        tiled=True,
    )
    return (owned_density, diag_density)


def solution(mesh):
    placed = (
        P("pole", None, "leaf", None),
        P("pole", "leaf", None),
        P("pole", None, None),
        P("pole", None),
        P(),
        P("leaf", None),
    )
    return jax.shard_map(
        body, mesh=mesh, in_specs=placed, out_specs=(P("leaf", None, None), P()), check_vma=False
    )
```

profile of v0, /device:TPU:1, one launch (start us, length us, event | category | flops | bytes accessed | tf_op | source)
XLA Modules:
  0.0 519.0 jit_solution(18408811787066555844)
XLA Ops:
  7.2 0.7 all-gather.2.cloned.1.call-update
  8.0 0.7 select_reduce_fusion.1
  8.7 0.9 select_reduce_fusion
  9.6 1.1 convert_multiply_fusion
  10.7 105.5 %all-gather.2.cloned.1.call-done = bf16[1,8192,512]{2,1,0:T(8,128)(2,1)} async-done(((bf16[1,256,512]{2,1,0:T(8,128)(2,1)}), bf16[1,8192,512]{2,1,0:T(8,128)(2,1)}) %all-gather.2.cloned.1.call-update) | async-done | bytes 8388624 | tf_op jit(solution)/shard_map/all_gather | solution.py:23
  116.2 10.4 %fusion.5 = f32[1,2,256,512]{3,2,1,0:T(8,128)S(1)} fusion(bf16[1,2,256,8192]{3,2,1,0:T(8,128)(2,1)} %param.6, bf16[1,8192,512]{2,1,0:T(8,128)(2,1)} %all-gather.2.cloned.1.call-done, bf16[8192]{0:T(1024)(128)(2,1)S(1)} %convert_convert_fusion), kind=kOutput, calls=%fused_computation.6 | convolution fusion | flops 4311744512 | bytes 17842176 | tf_op jit(solution)/shard_map/pcrk,pkn->pcrn/dot_general | solution.py:15
  126.6 0.7 fusion.18
  127.2 0.7 fusion.22
  127.9 1.4 fusion.10
  129.3 1.4 fusion.11
  130.7 0.0 all-reduce.7.cloned.1.call-start
  130.8 0.1 convert_element_type.34
  130.8 0.6 fusion.41
  131.4 2.0 fusion.26
  133.4 262.7 %all-reduce.5.cloned.1.call-done = (f32[1,256,256]{2,1,0:T(8,128)}, f32[1,256,256]{2,1,0:T(8,128)}) async-done(((f32[1,256,256]{2,1,0:T(8,128)}, f32[1,256,256]{2,1,0:T(8,128)}), (f32[1,256,256]{2,1,0:T(8,128)}, f32[1,256,256]{2,1,0:T(8,128)})) %all-reduce.5.cloned.1.call-update) | async-done | bytes 524304 | tf_op jit(solution)/shard_map/psum | solution.py:45
  396.1 3.0 fusion.14
  399.2 0.1 fusion.35
  399.3 0.1 reduce_window_sum.11
  399.3 0.2 select_reduce_fusion.2
  399.5 74.7 %all-reduce.7.cloned.1.call-done = (f32[32,8,256]{2,1,0:T(8,128)}, f32[256,256]{1,0:T(8,128)}) async-done(((f32[32,8,256]{2,1,0:T(8,128)}, f32[256,256]{1,0:T(8,128)}), (f32[32,8,256]{2,1,0:T(8,128)}, f32[256,256]{1,0:T(8,128)})) %all-reduce.7.cloned.1.call-update) | async-done | bytes 524304 | tf_op jit(solution)/shard_map/psum | solution.py:57
  474.3 2.8 scatter_fusion
  477.1 32.8 %all_to_all.5 = f32[64,8,256]{2,1,0:T(8,128)S(1)} all-to-all(f32[64,8,256]{2,1,0:T(8,128)S(1)} %scatter_fusion), channel_id=1, replica_groups=mesh['pole'=8,'leaf'=32] {'leaf'}, dimensions={0} | all-to-all | bytes 1048576 | tf_op jit(solution)/shard_map/all_to_all | solution.py:61
  510.0 0.8 copy.14
  510.8 1.7 copy.15
  (16 shorter events, 0.2 us)
Async XLA Ops:
  7.2 109.0 %all-gather.2.cloned.1.call-start = ((), (), s32[]{:S(2)}) async-start(), calls=%async_computation.1 | async-start | bytes 8650752 | tf_op jit(solution)/shard_map/all_gather | solution.py:23
  7.9 388.2 %all-reduce.5.cloned.1.call-start = ((), (), s32[]{:S(2)}) async-start(), calls=%async_computation.2 | async-start | bytes 1048576 | tf_op jit(solution)/shard_map/psum | solution.py:45
  10.7 120.0 %copy-start = (bf16[1,256,512]{2,1,0:T(8,128)(2,1)S(1)}, bf16[1,256,512]{2,1,0:T(8,128)(2,1)}, u32[]{:S(2)}) copy-start(bf16[1,256,512]{2,1,0:T(8,128)(2,1)} %param.8) | copy-start | bytes 786436
  10.7 120.1 %copy-start.2 = (f32[1,2]{1,0:T(1,128)S(1)}, f32[1,2]{1,0:T(1,128)}, u32[]{:S(2)}) copy-start(f32[1,2]{1,0:T(1,128)} %param.9) | copy-start | bytes 28
  10.7 388.4 %copy-start.1 = (s32[32,1]{0,1:T(1,128)S(1)}, s32[32,1]{0,1:T(1,128)}, u32[]{:S(2)}) copy-start(s32[32,1]{0,1:T(1,128)} %param.11) | copy-start | bytes 388
  130.7 343.5 %all-reduce.7.cloned.1.call-start = ((), (), s32[]{:S(2)}) async-start(), calls=%async_computation.3 | async-start | bytes 1048576 | tf_op jit(solution)/shard_map/psum | solution.py:57
Sparse Core Ops, SparseCore 0:
  10.7 105.4 all-gather.1
  130.8 265.2 all-reduce.4
  399.4 74.7 all-reduce.6
where the time goes:
time: 519 us
  waiting for transfers between devices  444 us (86%)
  blocking collectives  32.8 us (6%)
  matrix products  14.4 us (3%)
  between operations  13.9 us (3%)
  other arithmetic  8.1 us (2%)
  local copies, waits for them, and re-layouts  5.93 us (1%)
    psum x1, waiting for transfers between devices, body(): schur_real, schur_imag = lax.psum((schur_real, schur_imag), 'leaf')  263 us
    all_gather x1, waiting for transfers between devices, body(): panel_rows = lax.all_gather(factor_panel, 'leaf', axis=1, tiled=True)  105 us
    psum x1, waiting for transfers between devices, body(): density_rows = lax.psum(density_part, 'pole')  74.7 us
    all_to_all x1, blocking collectives, body(): lax.all_to_all(buffer_zero.at[slot_index].set(element_blocks), 'leaf', sp...  32.8 us
  transfers between devices with their start and end apart: 3, of which 3 were waited for; matrix products, arithmetic and copies ran while one was open for 1% of the time, Pallas kernels for 0%

commit v1 on v0

v1 whole, which is shorter than its diff:
```python
import jax
import jax.numpy as jnp
from jax import lax
from jax.experimental import pallas as pl
from jax.experimental.pallas import tpu as pltpu
from jax.sharding import Mesh, PartitionSpec as P


LEAF = ("xh", "z", "c")
PLANE = ("pole", "xh", "c")
XH, Z, C, POLES = 2, 8, 2, 8
LEAVES = XH * Z * C
SN = 256
HALF = SN // 2
QUARTER = SN // 4
PLANES = 32
SOURCES = 4
RB = 8
BLOCKS = 32
SEL = 16
F32 = jnp.float32
BF16 = jnp.bfloat16


def leaf_perm(move):
    pairs = []
    for xh in range(XH):
        for z in range(Z):
            for c in range(C):
                a, b, d = move(xh, z, c)
                pairs.append(((xh * Z + z) * C + c, ((a % XH) * Z + b % Z) * C + d % C))
    return pairs


Z_FORTH = leaf_perm(lambda xh, z, c: (xh, z + 1 - 2 * c, c))
Z_BACK = leaf_perm(lambda xh, z, c: (xh, z - 1 + 2 * c, c))
X_SWAP = leaf_perm(lambda xh, z, c: (xh + 1, z, c))
DIAGONAL = leaf_perm(lambda xh, z, c: (xh + 1, z + 1 - 2 * c, c))
C_SWAP = leaf_perm(lambda xh, z, c: (xh, z, c + 1))


PANELS = (
    ("own", 0, 0),
    ("b1", 1, 0),
    ("x0", 0, 1),
    ("f1", -1, 0),
    ("f2", -2, 0),
    ("b2", 2, 0),
    ("y1", 1, 1),
    ("x1", -1, 1),
    ("f3", -3, 0),
    ("b3", 3, 0),
    ("y2", 2, 1),
    ("x2", -2, 1),
    ("f4", -4, 0),
    ("y3", 3, 1),
    ("x3", -3, 1),
    ("x4", -4, 1),
)


def send(value, perm):
    return lax.ppermute(value, LEAF, perm)


def vmem():
    return pl.BlockSpec(memory_space=pltpu.VMEM)


def room(mib):
    return pltpu.CompilerParams(vmem_limit_bytes=mib << 20)


def near(shape, kind=F32):
    return pltpu.VMEM(shape, kind)


def held(*values):
    return [pltpu.with_memory_space_constraint(value, pltpu.VMEM) for value in values]


def smem():
    return pl.BlockSpec(memory_space=pltpu.SMEM)


def lane_places(structure_ref, xh, z, lane):
    places, count = [], jnp.int32(0)
    for _, dz, dx in PANELS:
        leaf = (((xh + dx) & (XH - 1)) * Z + ((z + (1 - 2 * lane) * dz) & (Z - 1))) * C + lane
        kept = structure_ref[leaf]
        places.append((leaf, kept, count))
        count = count + kept
    return places


def pick_kernel(structure_ref, front_ref, keep_ref, give_ref, sems):
    xh, z, c = (lax.axis_index(name) for name in LEAF)
    copies = []
    for which, (lane, out_ref) in enumerate(((c, keep_ref), (1 - c, give_ref))):
        for leaf, kept, count in lane_places(structure_ref, xh, z, lane):
            copy = pltpu.make_async_copy(
                front_ref.at[0, :, :, pl.ds(pl.multiple_of(leaf * SN, SN), SN)],
                out_ref.at[count],
                sems.at[which, count],
            )
            copies.append((kept, copy))
    for kept, copy in copies:
        pl.when(kept == 1)(copy.start)
    for kept, copy in copies:
        pl.when(kept == 1)(copy.wait)


def pick_front(structure, front):
    return pl.pallas_call(
        pick_kernel,
        in_specs=[smem(), pl.BlockSpec(memory_space=pltpu.HBM)],
        out_specs=[vmem(), vmem()],
        out_shape=[near((SEL, 2, SN, SN), BF16)] * 2,
        scratch_shapes=[pltpu.SemaphoreType.DMA((2, SEL))],
        compiler_params=room(2),
        name="pick_front",
    )(structure, pltpu.with_memory_space_constraint(front, pltpu.HBM))


def add_products(structure_ref, keep_ref, got_ref, acc_ref, pieces):
    all_places = lane_places(structure_ref, *(lax.axis_index(name) for name in LEAF))
    for piece, places in pieces:
        for half, place in enumerate(places):

            _, kept, count = all_places[place]

            @pl.when(kept == 1)
            def _(piece=piece, half=half, count=count):
                panel = piece[half * SN : (half + 1) * SN, :]
                for k, front_ref in enumerate((keep_ref, got_ref)):
                    acc_ref[k] += jnp.dot(
                        front_ref[count].reshape(2 * SN, SN), panel, preferred_element_type=F32
                    )


def partial_product(structure, keep, got, acc, pieces, places):
    given = 0 if acc is None else 1

    def kernel(structure_ref, keep_ref, got_ref, *refs):
        out_ref = refs[-1]
        out_ref[...] = refs[0][...] if given else jnp.zeros_like(out_ref)
        add_products(structure_ref, keep_ref, got_ref, out_ref, list(zip(refs[given:-1], places)))

    return pl.pallas_call(
        kernel,
        in_specs=[smem()] + [vmem()] * (2 + given + len(pieces)),
        out_specs=vmem(),
        out_shape=near((2, 2 * SN, 2 * SN)),
        input_output_aliases={3: 0} if given else {},
        compiler_params=room(4),
        name="partial_product",
    )(structure, *held(keep, got, *([acc] if given else []), *pieces))


def low_lanes(shape):
    return lax.broadcasted_iota(jnp.int32, shape, 1) < QUARTER


def turned(value):
    return pltpu.roll(value, QUARTER, 1)


def pack(out_ref, g, low, first, second):
    count = first.shape[0]
    out_ref[g, :count] = jnp.where(low, first, turned(second))
    out_ref[g + 1, :count] = jnp.where(low, turned(first), second)


def last_product(structure, weight, keep, got, acc, pieces, places):
    def kernel(structure_ref, weight_ref, keep_ref, got_ref, acc_in, *refs):
        own_ref, other_ref, acc_ref = refs[-3:]
        acc_ref[...] = acc_in[...]
        add_products(structure_ref, keep_ref, got_ref, acc_ref, list(zip(refs[:-3], places)))
        wr = weight_ref[0, 0]
        wi = weight_ref[0, 1]
        for k, out_ref in enumerate((own_ref, other_ref)):
            block_real = acc_ref[k, SN:, SN:] - acc_ref[k, :SN, :SN]
            block_imag = -(acc_ref[k, :SN, SN:] + acc_ref[k, SN:, :SN])
            out_ref[0] = wr * block_imag + wi * block_real
            out_ref[1] = wr * block_real - wi * block_imag

    return pl.pallas_call(
        kernel,
        in_specs=[smem(), smem()] + [vmem()] * (3 + len(pieces)),
        out_specs=[vmem(), vmem()],
        out_shape=[near((2, SN, SN))] * 2,
        scratch_shapes=[pltpu.VMEM((2, 2 * SN, 2 * SN), F32)],
        compiler_params=room(8),
        name="last_product",
    )(structure, weight, *held(keep, got, acc, *pieces))


def three_parts(value):
    first = value.astype(BF16)
    rest = value - first.astype(F32)
    second = rest.astype(BF16)
    return first, second, (rest - second.astype(F32)).astype(BF16)


def weigh(structure, weight, own, other, panel, diag):
    def kernel(structure_ref, weight_ref, own_ref, other_ref, panel_ref, diag_ref, out_ref, den_ref, cor_ref):
        xh, z, c = (lax.axis_index(name) for name in LEAF)
        leaf = (xh * Z + z) * C + c
        row = structure_ref[leaf].astype(F32)
        lead = (leaf == 0).astype(F32)
        wr = weight_ref[0, 0]
        wi = weight_ref[0, 1]
        density = (own_ref[0] + other_ref[0]) * row
        other = (own_ref[1] + other_ref[1]) * row
        den_ref[0] = density[:, :HALF]
        den_ref[1] = density[:, HALF:]
        schur = jnp.zeros((SN, SN), F32)
        for left, parts in ((panel_ref[:, :SN], three_parts(density)), (panel_ref[:, SN:], three_parts(other))):
            for part in parts:
                schur += lax.dot_general(left, part, (((0,), (0,)), ((), ())), preferred_element_type=F32)
        diag_real = diag_ref[0, :, :SN].astype(F32)
        diag_imag = diag_ref[0, :, SN:].astype(F32)
        cor_ref[...] = lead * (wr * diag_imag + wi * diag_real) - schur
        low = low_lanes((BLOCKS // 2, HALF))
        for q in range(POLES):
            for x in range(XH):
                rows = den_ref[x, pl.ds(q, BLOCKS, stride=RB), :]
                pack(out_ref, (q * XH + x) * C, low, rows[: BLOCKS // 2], rows[BLOCKS // 2 :])
        for g in range(PLANES):
            out_ref[g, 16:24] = cor_ref[8 * g : 8 * g + 8, :HALF]
            out_ref[g, 24:] = cor_ref[8 * g : 8 * g + 8, HALF:]

    return pl.pallas_call(
        kernel,
        in_specs=[smem(), smem()] + [vmem()] * 4,
        out_specs=vmem(),
        out_shape=near((PLANES, 32, HALF)),
        scratch_shapes=[pltpu.VMEM((XH, SN, HALF), F32), pltpu.VMEM((SN, SN), F32)],
        compiler_params=room(6),
        name="weigh",
    )(structure, weight, *held(own, other, panel), diag)


def route_kernel(near_ref, far_ref, got_ref, out_ref, row_ref):
    corner = got_ref[0, 16:]
    for g in range(1, PLANES):
        corner += got_ref[g, 16:]
    for source in range(SOURCES):
        rows = got_ref[source, :16]
        for q in range(1, POLES):
            rows += got_ref[q * SOURCES + source, :16]
        other = turned(rows)
        row_ref[0, source * BLOCKS : source * BLOCKS + 16] = rows
        row_ref[0, source * BLOCKS + 16 : source * BLOCKS + 32] = other
        row_ref[1, source * BLOCKS : source * BLOCKS + 16] = other
        row_ref[1, source * BLOCKS + 16 : source * BLOCKS + 32] = rows
    for z in range(Z):
        out_ref[z, :16] = jnp.zeros((16, HALF), F32)
        out_ref[z, 16:] = corner
    xh, c = lax.axis_index("xh"), lax.axis_index("c")
    high = lax.broadcasted_iota(jnp.int32, (1, HALF), 1) // QUARTER
    for dx, places in enumerate((near_ref, far_ref)):
        for dc in range(C):
            source = (xh ^ dx) * C + (c ^ dc)
            for b in range(BLOCKS):
                place = places[dc, b]
                rank = place & 1
                row = pl.ds(((place >> 1) & 15) + source, 1)
                taken = row_ref[rank, pl.ds(source * BLOCKS + b, 1), :]
                z = place >> 5
                out_ref[z, row, :] = jnp.where(high == rank, taken, out_ref[z, row, :])


def route(here, there, got):
    return pl.pallas_call(
        route_kernel,
        in_specs=[smem(), smem(), vmem()],
        out_specs=vmem(),
        out_shape=near((Z, 32, HALF)),
        scratch_shapes=[pltpu.VMEM((2, SOURCES * BLOCKS, HALF), F32)],
        compiler_params=room(4),
        name="route",
    )(here, there, *held(got))


def spread_kernel(structure_ref, got_ref, out_ref, row_ref):
    corner = got_ref[0, 16:]
    for z in range(1, Z):
        corner += got_ref[z, 16:]
    count = jnp.int32(0)
    for leaf in range(LEAVES):

        @pl.when(structure_ref[leaf] == 1)
        def _(leaf=leaf, count=count):
            source = (leaf // (Z * C)) * C + leaf % C
            for owner in range(SOURCES):
                row = owner * SOURCES + source
                row_ref[owner, pl.ds(count, 1), :] = got_ref[(leaf // C) % Z, row : row + 1, :]

        count = count + structure_ref[leaf]
    for owner in range(SOURCES):
        rows = row_ref[owner]
        for q in range(POLES):
            out_ref[q * SOURCES + owner, :SEL] = rows
    for g in range(PLANES):
        out_ref[g, SEL:] = corner


def spread(structure, got):
    return pl.pallas_call(
        spread_kernel,
        in_specs=[smem(), vmem()],
        out_specs=vmem(),
        out_shape=near((PLANES, SEL + 16, HALF)),
        scratch_shapes=[pltpu.VMEM((SOURCES, SEL, HALF), F32)],
        compiler_params=room(4),
        name="spread",
    )(structure, *held(got))


def finish_kernel(structure_ref, got_ref, owned_ref, diag_ref, row_ref):
    low = low_lanes((SEL, HALF))
    for q in range(POLES):
        for x in range(XH):
            g = (q * XH + x) * C
            first, second = got_ref[g, :SEL], got_ref[g + 1, :SEL]
            row_ref[x, pl.ds(q, SEL, stride=2 * RB), :] = jnp.where(low, first, turned(second))
            row_ref[x, pl.ds(q + RB, SEL, stride=2 * RB), :] = jnp.where(low, turned(first), second)
    for g in range(PLANES):
        diag_ref[8 * g : 8 * g + 8, :HALF] = got_ref[g, SEL : SEL + 8]
        diag_ref[8 * g : 8 * g + 8, HALF:] = got_ref[g, SEL + 8 :]
    count = jnp.int32(0)
    for leaf in range(LEAVES):
        place = slice(leaf * 2 * RB, (leaf + 1) * 2 * RB)

        @pl.when(structure_ref[leaf] == 1)
        def _(place=place, count=count):
            for x in range(XH):
                owned_ref[place, x * HALF : (x + 1) * HALF] = row_ref[
                    x, pl.ds(pl.multiple_of(count * 2 * RB, 2 * RB), 2 * RB), :
                ]

        @pl.when(structure_ref[leaf] != 1)
        def _(place=place):
            owned_ref[place] = jnp.zeros((2 * RB, SN), F32)

        count = count + structure_ref[leaf]


def finish(structure, got):
    return pl.pallas_call(
        finish_kernel,
        in_specs=[smem(), vmem()],
        out_specs=[vmem(), vmem()],
        out_shape=[jax.ShapeDtypeStruct((64 * RB, SN), F32), jax.ShapeDtypeStruct((SN, SN), F32)],
        scratch_shapes=[pltpu.VMEM((XH, SEL * 2 * RB, HALF), F32)],
        compiler_params=room(6),
        name="finish",
    )(structure, *held(got))


def body(inverse_front, factor_panel, diag_inverse, pole_weight, structure, block_owner):
    xh, z, c = (lax.axis_index(name) for name in LEAF)
    own = factor_panel[0]

    ids = jnp.arange(LEAVES, dtype=jnp.int32)
    owners = block_owner[:, 0]
    same = (owners[:, None] == owners[None, :]) & (ids[None, :] < ids[:, None])
    rank = jnp.sum(same.astype(jnp.int32), axis=1)
    member = (owners // (Z * C)) * C + owners % C
    place = (((owners // C) % Z) * 16 + member * SOURCES) * 2 + rank
    here = jnp.stack([place, send(place, C_SWAP)])
    there = send(here, X_SWAP)

    keep, give = pick_front(structure, inverse_front)
    got = send(give, C_SWAP)

    f1 = send(own, Z_FORTH)
    b1 = send(own, Z_BACK)
    x0 = send(own, X_SWAP)
    f2 = send(f1, Z_FORTH)
    b2 = send(b1, Z_BACK)
    y1 = send(x0, Z_BACK)
    x1 = send(f1, X_SWAP)
    f3 = send(f2, Z_FORTH)
    b3 = send(b2, Z_BACK)
    y2 = send(y1, Z_BACK)
    x2 = send(f2, X_SWAP)
    f4 = send(f3, Z_FORTH)
    y3 = send(y2, Z_BACK)
    x3 = send(f3, X_SWAP)
    x4 = send(f3, DIAGONAL)

    acc = partial_product(structure, keep, got, None, [own, b1, x0, f1], [(0,), (1,), (2,), (3,)])
    acc = partial_product(structure, keep, got, acc, [f2, b2, y1, x1], [(4,), (5,), (6,), (7,)])
    acc = partial_product(structure, keep, got, acc, [f3, b3, y2, x2], [(8,), (9,), (10,), (11,)])
    late, there = lax.optimization_barrier((structure, there))
    mine, theirs = last_product(
        late, pole_weight, keep, got, acc, [f4, y3, x3, x4], [(12,), (13,), (14,), (15,)]
    )
    theirs = send(theirs, C_SWAP)
    parts = weigh(structure, pole_weight, mine, theirs, own, diag_inverse)
    parts = lax.all_to_all(parts, PLANE, 0, 0, tiled=True)
    parts = lax.all_to_all(route(here, there, parts), "z", 0, 0, tiled=True)
    parts = lax.all_to_all(spread(structure, parts), PLANE, 0, 0, tiled=True)
    owned, diag = finish(structure, parts)
    return owned.reshape(64, RB, SN), diag


def solution(mesh):
    split = Mesh(mesh.devices.reshape(POLES, XH, Z, C), ("pole", "xh", "z", "c"))
    placed = (
        P("pole", None, LEAF, None),
        P("pole", LEAF, None),
        P("pole", None, None),
        P("pole", None),
        P(),
        P(LEAF, None),
    )
    return jax.shard_map(
        body, mesh=split, in_specs=placed, out_specs=(P(LEAF, None, None), P()), check_vma=False
    )
```

time: 519 us -> 113 us (0.22)
  waiting for transfers between devices: 444 us -> 13.7 us
  starting transfers between devices: 0.12 us -> 33.9 us
  Pallas kernels: 0 us -> 15.7 us
  blocking collectives: 32.8 us -> 47.3 us
  matrix products: 14.4 us -> 0 us
  between operations: 13.9 us -> 0.79 us
  other arithmetic: 8.1 us -> 0.23 us
  local copies, waits for them, and re-layouts: 5.93 us -> 0.71 us
    psum x2 -> x0, waiting for transfers between devices: 337 us -> none  [the longest x1 263 us: body(): schur_real, schur_imag = lax.psum((schur_real, schur_imag), 'leaf')]
    all_gather x1 -> x0, waiting for transfers between devices: 105 us -> none  [body(): panel_rows = lax.all_gather(factor_panel, 'leaf', axis=1, tiled=True)]
    ppermute x0 -> x19, starting transfers between devices: none -> 33.9 us  [send(): return lax.ppermute(value, LEAF, perm)]
    pallas_call x0 -> x9, Pallas kernels: none -> 15.7 us  [the longest x3 5.85 us: partial_product(): pl.pallas_call(kernel, in_specs=[smem()] + [vmem()] * (2 + given + len(pi...]
    all_to_all x1 -> x3, blocking collectives: 32.8 us -> 47.3 us  [the longest x1 18 us: body(): parts = lax.all_to_all(parts, PLANE, 0, 0, tiled=True)]
    dot_general x5 -> x0, matrix products: 14.4 us -> none  [the longest x1 10.4 us: panel_product(): jnp.einsum('pcrk,pkn->pcrn', columns, panel, preferred_element_type=jnp.f...]
    ppermute x0 -> x19, waiting for transfers between devices: none -> 13.7 us  [send(): return lax.ppermute(value, LEAF, perm)]
  transfers between devices with their start and end apart: 3 -> 19, of which waited for: 3 -> 8; matrix products, arithmetic and copies ran while one was open for 1% -> 0% of each run, Pallas kernels for 0% -> 5%
where the time goes in v1:
time: 113 us; the launch traced here: 112 us
  blocking collectives  47.3 us (42%)
  starting transfers between devices  33.9 us (30%)
  Pallas kernels  15.7 us (14%)
  waiting for transfers between devices  13.7 us (12%)
    ppermute x19, starting transfers between devices, send(): return lax.ppermute(value, LEAF, perm)  33.9 us
    all_to_all x1, blocking collectives, body(): parts = lax.all_to_all(parts, PLANE, 0, 0, tiled=True)  18 us
    all_to_all x1, blocking collectives, body(): parts = lax.all_to_all(spread(structure, parts), PLANE, 0, 0, tiled=True)  16.5 us
    ppermute x19, waiting for transfers between devices, send(): return lax.ppermute(value, LEAF, perm)  13.7 us
    all_to_all x1, blocking collectives, body(): parts = lax.all_to_all(route(here, there, parts), 'z', 0, 0, tiled=True)  12.9 us
    pallas_call x3, Pallas kernels, partial_product(): pl.pallas_call(kernel, in_specs=[smem()] + [vmem()] * (2 + given + len(pi...  5.85 us
    pallas_call x1, Pallas kernels, pick_front(): pl.pallas_call(pick_kernel, in_specs=[smem(), pl.BlockSpec(memory_space=p...  3.07 us
  transfers between devices with their start and end apart: 19, of which 8 were waited for; matrix products, arithmetic and copies ran while one was open for 0% of the time, Pallas kernels for 5%

profile of v1, /device:TPU:1, one launch (start us, length us, event | category | flops | bytes accessed | tf_op | source)
XLA Modules:
  0.0 112.5 jit_solution(8999969645148839708)
XLA Ops:
  1.3 3.1 %pick_front.1 = (bf16[16,2,256,256]{3,2,1,0:T(8,128)(2,1)S(1)}, bf16[16,2,256,256]{3,2,1,0:T(8,128)(2,1)S(1)}) custom-call(s32[32]{0:T(128)S(1)} %copy-done.2, bf16[1,2,256,8192]{3,2,1,0:T(8,128)(2,1)} %front_ref.1), custom_call_target="tpu_custom_call" | custom-call | tf_op jit(solution)/shard_map/pick_front/pallas_call | solution.py:114
  4.4 3.3 %collective-permute-start.2 = (bf16[16,2,256,256]{3,2,1,0:T(8,128)(2,1)S(1)}, bf16[16,2,256,256]{3,2,1,0:T(8,128)(2,1)S(1)}, u32[]{:S(2)}, u32[]{:S(2)}) collective-permute-start(bf16[16,2,256,256]{3,2,1,0:T(8,128)(2,1)S(1)} %get-tuple-element.13), channel_id=1, source_target_pairs={{0,1},{1,0},{2,3},{3,2},{4,5},{5,4},{6,7},{7,6},{8,9},{9,8},{10,11... | collective-permute-start | bytes 12582920 | tf_op jit(solution)/shard_map/ppermute | solution.py:63
  7.7 3.9 %collective-permute-start.5 = (bf16[256,512]{1,0:T(8,128)(2,1)S(1)}, bf16[256,512]{1,0:T(8,128)(2,1)S(1)}, u32[]{:S(2)}, u32[]{:S(2)}) collective-permute-start(bf16[256,512]{1,0:T(8,128)(2,1)S(1)} %bitcast.23), channel_id=1, source_target_pairs={{0,2},{1,15},{2,4},{3,1},{4,6},{5,3},{6,8},{7,5},{8,10},{9,7},{10,... | collective-permute-start | bytes 786440 | tf_op jit(solution)/shard_map/ppermute | solution.py:63
  11.6 2.7 %collective-permute-start.4 = (bf16[256,512]{1,0:T(8,128)(2,1)S(1)}, bf16[256,512]{1,0:T(8,128)(2,1)S(1)}, u32[]{:S(2)}, u32[]{:S(2)}) collective-permute-start(bf16[256,512]{1,0:T(8,128)(2,1)S(1)} %bitcast.25), channel_id=1, source_target_pairs={{0,16},{1,17},{2,18},{3,19},{4,20},{5,21},{6,22},{7,23},{8,24},{9,... | collective-permute-start | bytes 786440 | tf_op jit(solution)/shard_map/ppermute | solution.py:63
  15.4 1.7 %collective-permute-done.5.refs_3_ = bf16[256,512]{1,0:T(8,128)(2,1)S(1)} collective-permute-done((bf16[256,512]{1,0:T(8,128)(2,1)S(1)}, bf16[256,512]{1,0:T(8,128)(2,1)S(1)}, u32[]{:S(2)}, u32[]{:S(2)}) %collective-permute-start.5) | collective-permute-done | bytes 262176 | tf_op jit(solution)/shard_map/ppermute | solution.py:63
  17.1 3.4 %collective-permute-start.6 = (bf16[256,512]{1,0:T(8,128)(2,1)S(1)}, bf16[256,512]{1,0:T(8,128)(2,1)S(1)}, u32[]{:S(2)}, u32[]{:S(2)}) collective-permute-start(bf16[256,512]{1,0:T(8,128)(2,1)S(1)} %collective-permute-done.5.refs_3_), channel_id=1, source_target_pairs={{0,2},{1,15},{2,4},{3,1},{4,6},{5,3},{6,8},{7,5},{8,10},{9,7},{10,... | collective-permute-start | bytes 786440 | tf_op jit(solution)/shard_map/ppermute | solution.py:63
  20.6 2.8 %collective-permute-start.1 = (s32[2,32]{1,0:T(2,128)S(1)}, s32[2,32]{1,0:T(2,128)S(1)}, u32[]{:S(2)}, u32[]{:S(2)}) collective-permute-start(s32[2,32]{1,0:T(2,128)S(1)} %pad_add_fusion.near_ref), channel_id=1, source_target_pairs={{0,16},{1,17},{2,18},{3,19},{4,20},{5,21},{6,22},{7,23},{8,24},{9,... | collective-permute-start | bytes 776 | tf_op jit(solution)/shard_map/ppermute | solution.py:63
  24.6 3.0 %collective-permute-start.9 = (bf16[256,512]{1,0:T(8,128)(2,1)S(1)}, bf16[256,512]{1,0:T(8,128)(2,1)S(1)}, u32[]{:S(2)}, u32[]{:S(2)}) collective-permute-start(bf16[256,512]{1,0:T(8,128)(2,1)S(1)} %collective-permute-done.5.refs_3_), channel_id=1, source_target_pairs={{0,16},{1,17},{2,18},{3,19},{4,20},{5,21},{6,22},{7,23},{8,24},{9,... | collective-permute-start | bytes 786440 | tf_op jit(solution)/shard_map/ppermute | solution.py:63
  27.7 3.3 %collective-permute-start.10 = (bf16[256,512]{1,0:T(8,128)(2,1)S(1)}, bf16[256,512]{1,0:T(8,128)(2,1)S(1)}, u32[]{:S(2)}, u32[]{:S(2)}) collective-permute-start(bf16[256,512]{1,0:T(8,128)(2,1)S(1)} %collective-permute-done.6.refs_1_), channel_id=1, source_target_pairs={{0,2},{1,15},{2,4},{3,1},{4,6},{5,3},{6,8},{7,5},{8,10},{9,7},{10,... | collective-permute-start | bytes 786440 | tf_op jit(solution)/shard_map/ppermute | solution.py:63
  31.5 2.9 %collective-permute-done.10.refs_1_ = bf16[256,512]{1,0:T(8,128)(2,1)S(1)} collective-permute-done((bf16[256,512]{1,0:T(8,128)(2,1)S(1)}, bf16[256,512]{1,0:T(8,128)(2,1)S(1)}, u32[]{:S(2)}, u32[]{:S(2)}) %collective-permute-start.10) | collective-permute-done | bytes 262176 | tf_op jit(solution)/shard_map/ppermute | solution.py:63
  34.3 3.4 %collective-permute-start.14 = (bf16[256,512]{1,0:T(8,128)(2,1)S(1)}, bf16[256,512]{1,0:T(8,128)(2,1)S(1)}, u32[]{:S(2)}, u32[]{:S(2)}) collective-permute-start(bf16[256,512]{1,0:T(8,128)(2,1)S(1)} %collective-permute-done.10.refs_1_), channel_id=1, source_target_pairs={{0,2},{1,15},{2,4},{3,1},{4,6},{5,3},{6,8},{7,5},{8,10},{9,7},{10,... | collective-permute-start | bytes 786440 | tf_op jit(solution)/shard_map/ppermute | solution.py:63
  37.7 3.1 %collective-permute-done.13.refs_4_ = bf16[256,512]{1,0:T(8,128)(2,1)S(1)} collective-permute-done((bf16[256,512]{1,0:T(8,128)(2,1)S(1)}, bf16[256,512]{1,0:T(8,128)(2,1)S(1)}, u32[]{:S(2)}, u32[]{:S(2)}) %collective-permute-start.13) | collective-permute-done | bytes 262176 | tf_op jit(solution)/shard_map/ppermute | solution.py:63
  40.8 3.6 %collective-permute-start.17 = (bf16[256,512]{1,0:T(8,128)(2,1)S(1)}, bf16[256,512]{1,0:T(8,128)(2,1)S(1)}, u32[]{:S(2)}, u32[]{:S(2)}) collective-permute-start(bf16[256,512]{1,0:T(8,128)(2,1)S(1)} %collective-permute-done.10.refs_1_), channel_id=1, source_target_pairs={{0,18},{1,31},{2,20},{3,17},{4,22},{5,19},{6,24},{7,21},{8,26},{9,... | collective-permute-start | bytes 786440 | tf_op jit(solution)/shard_map/ppermute | solution.py:63
  45.0 1.6 %partial_product.3.refs_0_ = f32[2,512,512]{2,1,0:T(8,128)S(1)} custom-call(s32[32]{0:T(128)S(1)} %copy-done.3, bf16[16,2,256,256]{3,2,1,0:T(8,128)(2,1)S(1)} %get-tuple-element.12.keep_ref, bf16[16,2,256,256]{3,2,1,0:T(8,128)(2,1)S(1)} %collective-permute-done.2.got_ref, bf16[256,512]{1,0:T(8,128)(2,1)S(1)} %bitcast.26, ...), custom_call_target="tpu_custom_call" | custom-call | tf_op jit(solution)/shard_map/partial_product/pallas_call | solution.py:149
  46.6 2.1 %partial_product.4.refs_0_ = f32[2,512,512]{2,1,0:T(8,128)S(1)} custom-call(s32[32]{0:T(128)S(1)} %copy-done.3, bf16[16,2,256,256]{3,2,1,0:T(8,128)(2,1)S(1)} %get-tuple-element.12.keep_ref, bf16[16,2,256,256]{3,2,1,0:T(8,128)(2,1)S(1)} %collective-permute-done.2.got_ref, f32[2,512,512]{2,1,0:T(8,128)S(1)} %partial_product.3.refs_0_, ...), custom_call_target="tpu_custom_call", output_to_operand_aliasing={{}: (3, {})} | custom-call | tf_op jit(solution)/shard_map/partial_product/pallas_call | solution.py:149
  48.7 2.2 %partial_product.5.acc_in = f32[2,512,512]{2,1,0:T(8,128)S(1)} custom-call(s32[32]{0:T(128)S(1)} %copy-done.3, bf16[16,2,256,256]{3,2,1,0:T(8,128)(2,1)S(1)} %get-tuple-element.12.keep_ref, bf16[16,2,256,256]{3,2,1,0:T(8,128)(2,1)S(1)} %collective-permute-done.2.got_ref, f32[2,512,512]{2,1,0:T(8,128)S(1)} %partial_product.4.refs_0_, ...), custom_call_target="tpu_custom_call", output_to_operand_aliasing={{}: (3, {})} | custom-call | tf_op jit(solution)/shard_map/partial_product/pallas_call | solution.py:149
  51.8 2.2 %collective-permute-done.15.refs_1_ = bf16[256,512]{1,0:T(8,128)(2,1)S(1)} collective-permute-done((bf16[256,512]{1,0:T(8,128)(2,1)S(1)}, bf16[256,512]{1,0:T(8,128)(2,1)S(1)}, u32[]{:S(2)}, u32[]{:S(2)}) %collective-permute-start.15) | collective-permute-done | bytes 262176 | tf_op jit(solution)/shard_map/ppermute | solution.py:63
  54.0 1.7 %last_product.1 = (f32[2,256,256]{2,1,0:T(8,128)S(1)}, f32[2,256,256]{2,1,0:T(8,128)S(1)}) custom-call(s32[32]{0:T(128)S(1)} %copy-done.3, f32[1,2]{1,0:T(1,128)S(1)} %copy-done.4, bf16[16,2,256,256]{3,2,1,0:T(8,128)(2,1)S(1)} %get-tuple-element.12.keep_ref, bf16[16,2,256,256]{3,2,1,0:T(8,128)(2,1)S(1)} %collective-permute-done.2.got_ref, ...), custom_call_target="tpu_custom_call" | custom-call | tf_op jit(solution)/shard_map/last_product/pallas_call | solution.py:187
  55.8 2.7 %collective-permute-start.18 = (f32[2,256,256]{2,1,0:T(8,128)S(1)}, f32[2,256,256]{2,1,0:T(8,128)S(1)}, u32[]{:S(2)}, u32[]{:S(2)}) collective-permute-start(f32[2,256,256]{2,1,0:T(8,128)S(1)} %get-tuple-element.15), channel_id=1, source_target_pairs={{0,1},{1,0},{2,3},{3,2},{4,5},{5,4},{6,7},{7,6},{8,9},{9,8},{10,11... | collective-permute-start | bytes 1572872 | tf_op jit(solution)/shard_map/ppermute | solution.py:63
  58.5 1.5 %collective-permute-done.18.other_ref = f32[2,256,256]{2,1,0:T(8,128)S(1)} collective-permute-done((f32[2,256,256]{2,1,0:T(8,128)S(1)}, f32[2,256,256]{2,1,0:T(8,128)S(1)}, u32[]{:S(2)}, u32[]{:S(2)}) %collective-permute-start.18) | collective-permute-done | bytes 524320 | tf_op jit(solution)/shard_map/ppermute | solution.py:63
  61.0 18.0 %all_to_all.15.got_ref = f32[32,32,128]{2,1,0:T(8,128)S(1)} all-to-all(f32[32,32,128]{2,1,0:T(8,128)S(1)} %weigh.1), channel_id=1, replica_groups=mesh['pole'=8,'xh'=2,'z'=8,'c'=2] {'pole','xh','c'}, dimensions={0} | all-to-all | bytes 1048576 | tf_op jit(solution)/shard_map/all_to_all | solution.py:403
  80.2 12.9 %all_to_all.16.got_ref = f32[8,32,128]{2,1,0:T(8,128)S(1)} all-to-all(f32[8,32,128]{2,1,0:T(8,128)S(1)} %route.1), channel_id=1, replica_groups=mesh['pole'=8,'xh'=2,'z'=8,'c'=2] {'z'}, dimensions={0} | all-to-all | bytes 262144 | tf_op jit(solution)/shard_map/all_to_all | solution.py:404
  93.9 16.5 %all_to_all.17.got_ref = f32[32,32,128]{2,1,0:T(8,128)S(1)} all-to-all(f32[32,32,128]{2,1,0:T(8,128)S(1)} %spread.1), channel_id=1, replica_groups=mesh['pole'=8,'xh'=2,'z'=8,'c'=2] {'pole','xh','c'}, dimensions={0} | all-to-all | bytes 1048576 | tf_op jit(solution)/shard_map/all_to_all | solution.py:405
  110.4 2.0 %finish.1 = (f32[512,256]{1,0:T(8,128)}, f32[256,256]{1,0:T(8,128)}) custom-call(s32[32]{0:T(128)S(1)} %copy-done.3, f32[32,32,128]{2,1,0:T(8,128)S(1)} %all_to_all.17.got_ref), custom_call_target="tpu_custom_call" | custom-call | tf_op jit(solution)/shard_map/finish/pallas_call | solution.py:351
  (42 shorter events, 7.9 us)
Async XLA Ops:
  0.6 7.1 %copy-start = (bf16[1,256,512]{2,1,0:T(8,128)(2,1)S(1)}, bf16[1,256,512]{2,1,0:T(8,128)(2,1)}, u32[]{:S(2)}) copy-start(bf16[1,256,512]{2,1,0:T(8,128)(2,1)} %param.7) | copy-start | bytes 786436
  1.3 13.0 %copy-start.5 = (s32[32,1]{0,1:T(1,128)S(1)}, s32[32,1]{0,1:T(1,128)}, u32[]{:S(2)}) copy-start(s32[32,1]{0,1:T(1,128)} %param.11) | copy-start | bytes 388
  1.3 43.7 %copy-start.3 = (s32[32]{0:T(128)S(1)}, s32[32]{0:T(128)}, u32[]{:S(2)}) copy-start(s32[32]{0:T(128)} %structure_ref.14) | copy-start | bytes 388
  4.4 40.0 %collective-permute-start.2 = (bf16[16,2,256,256]{3,2,1,0:T(8,128)(2,1)S(1)}, bf16[16,2,256,256]{3,2,1,0:T(8,128)(2,1)S(1)}, u32[]{:S(2)}, u32[]{:S(2)}) collective-permute-start(bf16[16,2,256,256]{3,2,1,0:T(8,128)(2,1)S(1)} %get-tuple-element.13), channel_id=1, source_target_pairs={{0,1},{1,0},{2,3},{3,2},{4,5},{5,4},{6,7},{7,6},{8,9},{9,8},{10,11... | collective-permute-start | bytes 12582920 | tf_op jit(solution)/shard_map/ppermute | solution.py:63
  7.7 9.4 %collective-permute-start.5 = (bf16[256,512]{1,0:T(8,128)(2,1)S(1)}, bf16[256,512]{1,0:T(8,128)(2,1)S(1)}, u32[]{:S(2)}, u32[]{:S(2)}) collective-permute-start(bf16[256,512]{1,0:T(8,128)(2,1)S(1)} %bitcast.23), channel_id=1, source_target_pairs={{0,2},{1,15},{2,4},{3,1},{4,6},{5,3},{6,8},{7,5},{8,10},{9,7},{10,... | collective-permute-start | bytes 786440 | tf_op jit(solution)/shard_map/ppermute | solution.py:63
  11.6 8.9 %collective-permute-start.3 = (bf16[256,512]{1,0:T(8,128)(2,1)S(1)}, bf16[256,512]{1,0:T(8,128)(2,1)S(1)}, u32[]{:S(2)}, u32[]{:S(2)}) collective-permute-start(bf16[256,512]{1,0:T(8,128)(2,1)S(1)} %bitcast.24), channel_id=1, source_target_pairs={{0,14},{1,3},{2,0},{3,5},{4,2},{5,7},{6,4},{7,9},{8,6},{9,11},{10,... | collective-permute-start | bytes 786440 | tf_op jit(solution)/shard_map/ppermute | solution.py:63
  11.6 8.9 %collective-permute-start.4 = (bf16[256,512]{1,0:T(8,128)(2,1)S(1)}, bf16[256,512]{1,0:T(8,128)(2,1)S(1)}, u32[]{:S(2)}, u32[]{:S(2)}) collective-permute-start(bf16[256,512]{1,0:T(8,128)(2,1)S(1)} %bitcast.25), channel_id=1, source_target_pairs={{0,16},{1,17},{2,18},{3,19},{4,20},{5,21},{6,22},{7,23},{8,24},{9,... | collective-permute-start | bytes 786440 | tf_op jit(solution)/shard_map/ppermute | solution.py:63
  14.5 6.1 %collective-permute-start = (s32[32]{0:T(128)S(1)}, s32[32]{0:T(128)S(1)}, u32[]{:S(2)}, u32[]{:S(2)}) collective-permute-start(s32[32]{0:T(128)S(1)} %multiply_add_fusion), channel_id=1, source_target_pairs={{0,1},{1,0},{2,3},{3,2},{4,5},{5,4},{6,7},{7,6},{8,9},{9,8},{10,11... | collective-permute-start | bytes 392 | tf_op jit(solution)/shard_map/ppermute | solution.py:63
  17.1 10.6 %collective-permute-start.6 = (bf16[256,512]{1,0:T(8,128)(2,1)S(1)}, bf16[256,512]{1,0:T(8,128)(2,1)S(1)}, u32[]{:S(2)}, u32[]{:S(2)}) collective-permute-start(bf16[256,512]{1,0:T(8,128)(2,1)S(1)} %collective-permute-done.5.refs_3_), channel_id=1, source_target_pairs={{0,2},{1,15},{2,4},{3,1},{4,6},{5,3},{6,8},{7,5},{8,10},{9,7},{10,... | collective-permute-start | bytes 786440 | tf_op jit(solution)/shard_map/ppermute | solution.py:63
  20.5 10.5 %collective-permute-start.7 = (bf16[256,512]{1,0:T(8,128)(2,1)S(1)}, bf16[256,512]{1,0:T(8,128)(2,1)S(1)}, u32[]{:S(2)}, u32[]{:S(2)}) collective-permute-start(bf16[256,512]{1,0:T(8,128)(2,1)S(1)} %collective-permute-done.3.refs_1_), channel_id=1, source_target_pairs={{0,14},{1,3},{2,0},{3,5},{4,2},{5,7},{6,4},{7,9},{8,6},{9,11},{10,... | collective-permute-start | bytes 786440 | tf_op jit(solution)/shard_map/ppermute | solution.py:63
  20.5 10.8 %collective-permute-start.8 = (bf16[256,512]{1,0:T(8,128)(2,1)S(1)}, bf16[256,512]{1,0:T(8,128)(2,1)S(1)}, u32[]{:S(2)}, u32[]{:S(2)}) collective-permute-start(bf16[256,512]{1,0:T(8,128)(2,1)S(1)} %collective-permute-done.4.refs_2_), channel_id=1, source_target_pairs={{0,14},{1,3},{2,0},{3,5},{4,2},{5,7},{6,4},{7,9},{8,6},{9,11},{10,... | collective-permute-start | bytes 786440 | tf_op jit(solution)/shard_map/ppermute | solution.py:63
  20.6 4.0 %collective-permute-start.1 = (s32[2,32]{1,0:T(2,128)S(1)}, s32[2,32]{1,0:T(2,128)S(1)}, u32[]{:S(2)}, u32[]{:S(2)}) collective-permute-start(s32[2,32]{1,0:T(2,128)S(1)} %pad_add_fusion.near_ref), channel_id=1, source_target_pairs={{0,16},{1,17},{2,18},{3,19},{4,20},{5,21},{6,22},{7,23},{8,24},{9,... | collective-permute-start | bytes 776 | tf_op jit(solution)/shard_map/ppermute | solution.py:63
  24.6 6.8 %collective-permute-start.9 = (bf16[256,512]{1,0:T(8,128)(2,1)S(1)}, bf16[256,512]{1,0:T(8,128)(2,1)S(1)}, u32[]{:S(2)}, u32[]{:S(2)}) collective-permute-start(bf16[256,512]{1,0:T(8,128)(2,1)S(1)} %collective-permute-done.5.refs_3_), channel_id=1, source_target_pairs={{0,16},{1,17},{2,18},{3,19},{4,20},{5,21},{6,22},{7,23},{8,24},{9,... | collective-permute-start | bytes 786440 | tf_op jit(solution)/shard_map/ppermute | solution.py:63
  27.7 6.6 %collective-permute-start.10 = (bf16[256,512]{1,0:T(8,128)(2,1)S(1)}, bf16[256,512]{1,0:T(8,128)(2,1)S(1)}, u32[]{:S(2)}, u32[]{:S(2)}) collective-permute-start(bf16[256,512]{1,0:T(8,128)(2,1)S(1)} %collective-permute-done.6.refs_1_), channel_id=1, source_target_pairs={{0,2},{1,15},{2,4},{3,1},{4,6},{5,3},{6,8},{7,5},{8,10},{9,7},{10,... | collective-permute-start | bytes 786440 | tf_op jit(solution)/shard_map/ppermute | solution.py:63
  31.0 9.8 %collective-permute-start.13 = (bf16[256,512]{1,0:T(8,128)(2,1)S(1)}, bf16[256,512]{1,0:T(8,128)(2,1)S(1)}, u32[]{:S(2)}, u32[]{:S(2)}) collective-permute-start(bf16[256,512]{1,0:T(8,128)(2,1)S(1)} %collective-permute-done.6.refs_1_), channel_id=1, source_target_pairs={{0,16},{1,17},{2,18},{3,19},{4,20},{5,21},{6,22},{7,23},{8,24},{9,... | collective-permute-start | bytes 786440 | tf_op jit(solution)/shard_map/ppermute | solution.py:63
  31.3 9.6 %collective-permute-start.12 = (bf16[256,512]{1,0:T(8,128)(2,1)S(1)}, bf16[256,512]{1,0:T(8,128)(2,1)S(1)}, u32[]{:S(2)}, u32[]{:S(2)}) collective-permute-start(bf16[256,512]{1,0:T(8,128)(2,1)S(1)} %collective-permute-done.8.refs_3_), channel_id=1, source_target_pairs={{0,14},{1,3},{2,0},{3,5},{4,2},{5,7},{6,4},{7,9},{8,6},{9,11},{10,... | collective-permute-start | bytes 786440 | tf_op jit(solution)/shard_map/ppermute | solution.py:63
  31.5 17.3 %collective-permute-start.11 = (bf16[256,512]{1,0:T(8,128)(2,1)S(1)}, bf16[256,512]{1,0:T(8,128)(2,1)S(1)}, u32[]{:S(2)}, u32[]{:S(2)}) collective-permute-start(bf16[256,512]{1,0:T(8,128)(2,1)S(1)} %collective-permute-done.7.refs_2_), channel_id=1, source_target_pairs={{0,14},{1,3},{2,0},{3,5},{4,2},{5,7},{6,4},{7,9},{8,6},{9,11},{10,... | collective-permute-start | bytes 786440 | tf_op jit(solution)/shard_map/ppermute | solution.py:63
  34.3 16.6 %collective-permute-start.14 = (bf16[256,512]{1,0:T(8,128)(2,1)S(1)}, bf16[256,512]{1,0:T(8,128)(2,1)S(1)}, u32[]{:S(2)}, u32[]{:S(2)}) collective-permute-start(bf16[256,512]{1,0:T(8,128)(2,1)S(1)} %collective-permute-done.10.refs_1_), channel_id=1, source_target_pairs={{0,2},{1,15},{2,4},{3,1},{4,6},{5,3},{6,8},{7,5},{8,10},{9,7},{10,... | collective-permute-start | bytes 786440 | tf_op jit(solution)/shard_map/ppermute | solution.py:63
  40.8 10.9 %collective-permute-start.16 = (bf16[256,512]{1,0:T(8,128)(2,1)S(1)}, bf16[256,512]{1,0:T(8,128)(2,1)S(1)}, u32[]{:S(2)}, u32[]{:S(2)}) collective-permute-start(bf16[256,512]{1,0:T(8,128)(2,1)S(1)} %collective-permute-done.10.refs_1_), channel_id=1, source_target_pairs={{0,16},{1,17},{2,18},{3,19},{4,20},{5,21},{6,22},{7,23},{8,24},{9,... | collective-permute-start | bytes 786440 | tf_op jit(solution)/shard_map/ppermute | solution.py:63
  40.8 10.9 %collective-permute-start.17 = (bf16[256,512]{1,0:T(8,128)(2,1)S(1)}, bf16[256,512]{1,0:T(8,128)(2,1)S(1)}, u32[]{:S(2)}, u32[]{:S(2)}) collective-permute-start(bf16[256,512]{1,0:T(8,128)(2,1)S(1)} %collective-permute-done.10.refs_1_), channel_id=1, source_target_pairs={{0,18},{1,31},{2,20},{3,17},{4,22},{5,19},{6,24},{7,21},{8,26},{9,... | collective-permute-start | bytes 786440 | tf_op jit(solution)/shard_map/ppermute | solution.py:63
  44.5 9.5 %collective-permute-start.15 = (bf16[256,512]{1,0:T(8,128)(2,1)S(1)}, bf16[256,512]{1,0:T(8,128)(2,1)S(1)}, u32[]{:S(2)}, u32[]{:S(2)}) collective-permute-start(bf16[256,512]{1,0:T(8,128)(2,1)S(1)} %collective-permute-done.12.refs_3_), channel_id=1, source_target_pairs={{0,14},{1,3},{2,0},{3,5},{4,2},{5,7},{6,4},{7,9},{8,6},{9,11},{10,... | collective-permute-start | bytes 786440 | tf_op jit(solution)/shard_map/ppermute | solution.py:63
  48.7 5.3 %copy-start.4 = (f32[1,2]{1,0:T(1,128)S(1)}, f32[1,2]{1,0:T(1,128)}, u32[]{:S(2)}) copy-start(f32[1,2]{1,0:T(1,128)} %weight_ref.3) | copy-start | bytes 28
  50.9 9.1 %copy-start.1 = (bf16[1,256,512]{2,1,0:T(8,128)(2,1)S(1)}, bf16[1,256,512]{2,1,0:T(8,128)(2,1)}, u32[]{:S(2)}) copy-start(bf16[1,256,512]{2,1,0:T(8,128)(2,1)} %diag_ref.1) | copy-start | bytes 786436
  55.8 4.3 %collective-permute-start.18 = (f32[2,256,256]{2,1,0:T(8,128)S(1)}, f32[2,256,256]{2,1,0:T(8,128)S(1)}, u32[]{:S(2)}, u32[]{:S(2)}) collective-permute-start(f32[2,256,256]{2,1,0:T(8,128)S(1)} %get-tuple-element.15), channel_id=1, source_target_pairs={{0,1},{1,0},{2,3},{3,2},{4,5},{5,4},{6,7},{7,6},{8,9},{9,8},{10,11... | collective-permute-start | bytes 1572872 | tf_op jit(solution)/shard_map/ppermute | solution.py:63
  (1 other events, 0.7 us)

commit v2 on v1

--- a/solution.py
+++ b/solution.py
@@ -333,18 +333,12 @@
     for leaf in range(LEAVES):
         place = slice(leaf * 2 * RB, (leaf + 1) * 2 * RB)
 
-        @pl.when(structure_ref[leaf] == 1)
-        def _(place=place, count=count):
-            for x in range(XH):
-                owned_ref[place, x * HALF : (x + 1) * HALF] = row_ref[
-                    x, pl.ds(pl.multiple_of(count * 2 * RB, 2 * RB), 2 * RB), :
-                ]
-
-        @pl.when(structure_ref[leaf] != 1)
-        def _(place=place):
-            owned_ref[place] = jnp.zeros((2 * RB, SN), F32)
-
-        count = count + structure_ref[leaf]
+        kept = structure_ref[leaf]
+        start = pl.multiple_of(jnp.minimum(count, SEL - 1) * 2 * RB, 2 * RB)
+        for x in range(XH):
+            rows = row_ref[x, pl.ds(start, 2 * RB), :]
+            owned_ref[place, x * HALF : (x + 1) * HALF] = jnp.where(kept == 1, rows, 0.0)
+        count = count + kept
 
 
 def finish(structure, got):

time: 113 us -> 112 us (level)
  no operation moved by 1% of the time
where the time goes in v2:
time: 112 us
  blocking collectives  47.3 us (42%)
  starting transfers between devices  33.9 us (30%)
  Pallas kernels  15.3 us (14%)
  waiting for transfers between devices  13.7 us (12%)
    ppermute x19, starting transfers between devices, send(): return lax.ppermute(value, LEAF, perm)  33.9 us
    all_to_all x1, blocking collectives, body(): parts = lax.all_to_all(parts, PLANE, 0, 0, tiled=True)  18 us
    all_to_all x1, blocking collectives, body(): parts = lax.all_to_all(spread(structure, parts), PLANE, 0, 0, tiled=True)  16.5 us
    ppermute x19, waiting for transfers between devices, send(): return lax.ppermute(value, LEAF, perm)  13.7 us
    all_to_all x1, blocking collectives, body(): parts = lax.all_to_all(route(here, there, parts), 'z', 0, 0, tiled=True)  12.9 us
    pallas_call x3, Pallas kernels, partial_product(): pl.pallas_call(kernel, in_specs=[smem()] + [vmem()] * (2 + given + len(pi...  5.85 us
    pallas_call x1, Pallas kernels, pick_front(): pl.pallas_call(pick_kernel, in_specs=[smem(), pl.BlockSpec(memory_space=p...  3.07 us
  transfers between devices with their start and end apart: 19, of which 8 were waited for; matrix products, arithmetic and copies ran while one was open for 0% of the time, Pallas kernels for 5%

profile of v2, /device:TPU:1, one launch (start us, length us, event | category | flops | bytes accessed | tf_op | source)
XLA Modules:
  0.0 112.0 jit_solution(11266815747550106575)
XLA Ops:
  1.3 3.1 %pick_front.1 = (bf16[16,2,256,256]{3,2,1,0:T(8,128)(2,1)S(1)}, bf16[16,2,256,256]{3,2,1,0:T(8,128)(2,1)S(1)}) custom-call(s32[32]{0:T(128)S(1)} %copy-done.2, bf16[1,2,256,8192]{3,2,1,0:T(8,128)(2,1)} %front_ref.1), custom_call_target="tpu_custom_call" | custom-call | tf_op jit(solution)/shard_map/pick_front/pallas_call | solution.py:114
  4.4 3.3 %collective-permute-start.2 = (bf16[16,2,256,256]{3,2,1,0:T(8,128)(2,1)S(1)}, bf16[16,2,256,256]{3,2,1,0:T(8,128)(2,1)S(1)}, u32[]{:S(2)}, u32[]{:S(2)}) collective-permute-start(bf16[16,2,256,256]{3,2,1,0:T(8,128)(2,1)S(1)} %get-tuple-element.13), channel_id=1, source_target_pairs={{0,1},{1,0},{2,3},{3,2},{4,5},{5,4},{6,7},{7,6},{8,9},{9,8},{10,11... | collective-permute-start | bytes 12582920 | tf_op jit(solution)/shard_map/ppermute | solution.py:63
  7.7 3.9 %collective-permute-start.5 = (bf16[256,512]{1,0:T(8,128)(2,1)S(1)}, bf16[256,512]{1,0:T(8,128)(2,1)S(1)}, u32[]{:S(2)}, u32[]{:S(2)}) collective-permute-start(bf16[256,512]{1,0:T(8,128)(2,1)S(1)} %bitcast.23), channel_id=1, source_target_pairs={{0,2},{1,15},{2,4},{3,1},{4,6},{5,3},{6,8},{7,5},{8,10},{9,7},{10,... | collective-permute-start | bytes 786440 | tf_op jit(solution)/shard_map/ppermute | solution.py:63
  11.6 2.7 %collective-permute-start.4 = (bf16[256,512]{1,0:T(8,128)(2,1)S(1)}, bf16[256,512]{1,0:T(8,128)(2,1)S(1)}, u32[]{:S(2)}, u32[]{:S(2)}) collective-permute-start(bf16[256,512]{1,0:T(8,128)(2,1)S(1)} %bitcast.25), channel_id=1, source_target_pairs={{0,16},{1,17},{2,18},{3,19},{4,20},{5,21},{6,22},{7,23},{8,24},{9,... | collective-permute-start | bytes 786440 | tf_op jit(solution)/shard_map/ppermute | solution.py:63
  15.4 1.7 %collective-permute-done.5.refs_3_ = bf16[256,512]{1,0:T(8,128)(2,1)S(1)} collective-permute-done((bf16[256,512]{1,0:T(8,128)(2,1)S(1)}, bf16[256,512]{1,0:T(8,128)(2,1)S(1)}, u32[]{:S(2)}, u32[]{:S(2)}) %collective-permute-start.5) | collective-permute-done | bytes 262176 | tf_op jit(solution)/shard_map/ppermute | solution.py:63
  17.1 3.4 %collective-permute-start.6 = (bf16[256,512]{1,0:T(8,128)(2,1)S(1)}, bf16[256,512]{1,0:T(8,128)(2,1)S(1)}, u32[]{:S(2)}, u32[]{:S(2)}) collective-permute-start(bf16[256,512]{1,0:T(8,128)(2,1)S(1)} %collective-permute-done.5.refs_3_), channel_id=1, source_target_pairs={{0,2},{1,15},{2,4},{3,1},{4,6},{5,3},{6,8},{7,5},{8,10},{9,7},{10,... | collective-permute-start | bytes 786440 | tf_op jit(solution)/shard_map/ppermute | solution.py:63
  20.6 2.8 %collective-permute-start.1 = (s32[2,32]{1,0:T(2,128)S(1)}, s32[2,32]{1,0:T(2,128)S(1)}, u32[]{:S(2)}, u32[]{:S(2)}) collective-permute-start(s32[2,32]{1,0:T(2,128)S(1)} %pad_add_fusion.near_ref), channel_id=1, source_target_pairs={{0,16},{1,17},{2,18},{3,19},{4,20},{5,21},{6,22},{7,23},{8,24},{9,... | collective-permute-start | bytes 776 | tf_op jit(solution)/shard_map/ppermute | solution.py:63
  24.6 3.0 %collective-permute-start.9 = (bf16[256,512]{1,0:T(8,128)(2,1)S(1)}, bf16[256,512]{1,0:T(8,128)(2,1)S(1)}, u32[]{:S(2)}, u32[]{:S(2)}) collective-permute-start(bf16[256,512]{1,0:T(8,128)(2,1)S(1)} %collective-permute-done.5.refs_3_), channel_id=1, source_target_pairs={{0,16},{1,17},{2,18},{3,19},{4,20},{5,21},{6,22},{7,23},{8,24},{9,... | collective-permute-start | bytes 786440 | tf_op jit(solution)/shard_map/ppermute | solution.py:63
  27.7 3.3 %collective-permute-start.10 = (bf16[256,512]{1,0:T(8,128)(2,1)S(1)}, bf16[256,512]{1,0:T(8,128)(2,1)S(1)}, u32[]{:S(2)}, u32[]{:S(2)}) collective-permute-start(bf16[256,512]{1,0:T(8,128)(2,1)S(1)} %collective-permute-done.6.refs_1_), channel_id=1, source_target_pairs={{0,2},{1,15},{2,4},{3,1},{4,6},{5,3},{6,8},{7,5},{8,10},{9,7},{10,... | collective-permute-start | bytes 786440 | tf_op jit(solution)/shard_map/ppermute | solution.py:63
  31.5 2.9 %collective-permute-done.10.refs_1_ = bf16[256,512]{1,0:T(8,128)(2,1)S(1)} collective-permute-done((bf16[256,512]{1,0:T(8,128)(2,1)S(1)}, bf16[256,512]{1,0:T(8,128)(2,1)S(1)}, u32[]{:S(2)}, u32[]{:S(2)}) %collective-permute-start.10) | collective-permute-done | bytes 262176 | tf_op jit(solution)/shard_map/ppermute | solution.py:63
  34.3 3.4 %collective-permute-start.14 = (bf16[256,512]{1,0:T(8,128)(2,1)S(1)}, bf16[256,512]{1,0:T(8,128)(2,1)S(1)}, u32[]{:S(2)}, u32[]{:S(2)}) collective-permute-start(bf16[256,512]{1,0:T(8,128)(2,1)S(1)} %collective-permute-done.10.refs_1_), channel_id=1, source_target_pairs={{0,2},{1,15},{2,4},{3,1},{4,6},{5,3},{6,8},{7,5},{8,10},{9,7},{10,... | collective-permute-start | bytes 786440 | tf_op jit(solution)/shard_map/ppermute | solution.py:63
  37.7 3.1 %collective-permute-done.13.refs_4_ = bf16[256,512]{1,0:T(8,128)(2,1)S(1)} collective-permute-done((bf16[256,512]{1,0:T(8,128)(2,1)S(1)}, bf16[256,512]{1,0:T(8,128)(2,1)S(1)}, u32[]{:S(2)}, u32[]{:S(2)}) %collective-permute-start.13) | collective-permute-done | bytes 262176 | tf_op jit(solution)/shard_map/ppermute | solution.py:63
  40.8 3.6 %collective-permute-start.17 = (bf16[256,512]{1,0:T(8,128)(2,1)S(1)}, bf16[256,512]{1,0:T(8,128)(2,1)S(1)}, u32[]{:S(2)}, u32[]{:S(2)}) collective-permute-start(bf16[256,512]{1,0:T(8,128)(2,1)S(1)} %collective-permute-done.10.refs_1_), channel_id=1, source_target_pairs={{0,18},{1,31},{2,20},{3,17},{4,22},{5,19},{6,24},{7,21},{8,26},{9,... | collective-permute-start | bytes 786440 | tf_op jit(solution)/shard_map/ppermute | solution.py:63
  45.0 1.6 %partial_product.3.refs_0_ = f32[2,512,512]{2,1,0:T(8,128)S(1)} custom-call(s32[32]{0:T(128)S(1)} %copy-done.3, bf16[16,2,256,256]{3,2,1,0:T(8,128)(2,1)S(1)} %get-tuple-element.12.keep_ref, bf16[16,2,256,256]{3,2,1,0:T(8,128)(2,1)S(1)} %collective-permute-done.2.got_ref, bf16[256,512]{1,0:T(8,128)(2,1)S(1)} %bitcast.26, ...), custom_call_target="tpu_custom_call" | custom-call | tf_op jit(solution)/shard_map/partial_product/pallas_call | solution.py:149
  46.6 2.1 %partial_product.4.refs_0_ = f32[2,512,512]{2,1,0:T(8,128)S(1)} custom-call(s32[32]{0:T(128)S(1)} %copy-done.3, bf16[16,2,256,256]{3,2,1,0:T(8,128)(2,1)S(1)} %get-tuple-element.12.keep_ref, bf16[16,2,256,256]{3,2,1,0:T(8,128)(2,1)S(1)} %collective-permute-done.2.got_ref, f32[2,512,512]{2,1,0:T(8,128)S(1)} %partial_product.3.refs_0_, ...), custom_call_target="tpu_custom_call", output_to_operand_aliasing={{}: (3, {})} | custom-call | tf_op jit(solution)/shard_map/partial_product/pallas_call | solution.py:149
  48.7 2.2 %partial_product.5.acc_in = f32[2,512,512]{2,1,0:T(8,128)S(1)} custom-call(s32[32]{0:T(128)S(1)} %copy-done.3, bf16[16,2,256,256]{3,2,1,0:T(8,128)(2,1)S(1)} %get-tuple-element.12.keep_ref, bf16[16,2,256,256]{3,2,1,0:T(8,128)(2,1)S(1)} %collective-permute-done.2.got_ref, f32[2,512,512]{2,1,0:T(8,128)S(1)} %partial_product.4.refs_0_, ...), custom_call_target="tpu_custom_call", output_to_operand_aliasing={{}: (3, {})} | custom-call | tf_op jit(solution)/shard_map/partial_product/pallas_call | solution.py:149
  51.8 2.2 %collective-permute-done.15.refs_1_ = bf16[256,512]{1,0:T(8,128)(2,1)S(1)} collective-permute-done((bf16[256,512]{1,0:T(8,128)(2,1)S(1)}, bf16[256,512]{1,0:T(8,128)(2,1)S(1)}, u32[]{:S(2)}, u32[]{:S(2)}) %collective-permute-start.15) | collective-permute-done | bytes 262176 | tf_op jit(solution)/shard_map/ppermute | solution.py:63
  54.0 1.7 %last_product.1 = (f32[2,256,256]{2,1,0:T(8,128)S(1)}, f32[2,256,256]{2,1,0:T(8,128)S(1)}) custom-call(s32[32]{0:T(128)S(1)} %copy-done.3, f32[1,2]{1,0:T(1,128)S(1)} %copy-done.4, bf16[16,2,256,256]{3,2,1,0:T(8,128)(2,1)S(1)} %get-tuple-element.12.keep_ref, bf16[16,2,256,256]{3,2,1,0:T(8,128)(2,1)S(1)} %collective-permute-done.2.got_ref, ...), custom_call_target="tpu_custom_call" | custom-call | tf_op jit(solution)/shard_map/last_product/pallas_call | solution.py:187
  55.8 2.7 %collective-permute-start.18 = (f32[2,256,256]{2,1,0:T(8,128)S(1)}, f32[2,256,256]{2,1,0:T(8,128)S(1)}, u32[]{:S(2)}, u32[]{:S(2)}) collective-permute-start(f32[2,256,256]{2,1,0:T(8,128)S(1)} %get-tuple-element.15), channel_id=1, source_target_pairs={{0,1},{1,0},{2,3},{3,2},{4,5},{5,4},{6,7},{7,6},{8,9},{9,8},{10,11... | collective-permute-start | bytes 1572872 | tf_op jit(solution)/shard_map/ppermute | solution.py:63
  58.5 1.5 %collective-permute-done.18.other_ref = f32[2,256,256]{2,1,0:T(8,128)S(1)} collective-permute-done((f32[2,256,256]{2,1,0:T(8,128)S(1)}, f32[2,256,256]{2,1,0:T(8,128)S(1)}, u32[]{:S(2)}, u32[]{:S(2)}) %collective-permute-start.18) | collective-permute-done | bytes 524320 | tf_op jit(solution)/shard_map/ppermute | solution.py:63
  61.0 18.0 %all_to_all.15.got_ref = f32[32,32,128]{2,1,0:T(8,128)S(1)} all-to-all(f32[32,32,128]{2,1,0:T(8,128)S(1)} %weigh.1), channel_id=1, replica_groups=mesh['pole'=8,'xh'=2,'z'=8,'c'=2] {'pole','xh','c'}, dimensions={0} | all-to-all | bytes 1048576 | tf_op jit(solution)/shard_map/all_to_all | solution.py:397
  80.2 12.9 %all_to_all.16.got_ref = f32[8,32,128]{2,1,0:T(8,128)S(1)} all-to-all(f32[8,32,128]{2,1,0:T(8,128)S(1)} %route.1), channel_id=1, replica_groups=mesh['pole'=8,'xh'=2,'z'=8,'c'=2] {'z'}, dimensions={0} | all-to-all | bytes 262144 | tf_op jit(solution)/shard_map/all_to_all | solution.py:398
  93.9 16.5 %all_to_all.17.got_ref = f32[32,32,128]{2,1,0:T(8,128)S(1)} all-to-all(f32[32,32,128]{2,1,0:T(8,128)S(1)} %spread.1), channel_id=1, replica_groups=mesh['pole'=8,'xh'=2,'z'=8,'c'=2] {'pole','xh','c'}, dimensions={0} | all-to-all | bytes 1048576 | tf_op jit(solution)/shard_map/all_to_all | solution.py:399
  110.4 1.6 %finish.1 = (f32[512,256]{1,0:T(8,128)}, f32[256,256]{1,0:T(8,128)}) custom-call(s32[32]{0:T(128)S(1)} %copy-done.3, f32[32,32,128]{2,1,0:T(8,128)S(1)} %all_to_all.17.got_ref), custom_call_target="tpu_custom_call" | custom-call | tf_op jit(solution)/shard_map/finish/pallas_call | solution.py:345
  (42 shorter events, 7.9 us)
Async XLA Ops:
  0.6 7.1 %copy-start = (bf16[1,256,512]{2,1,0:T(8,128)(2,1)S(1)}, bf16[1,256,512]{2,1,0:T(8,128)(2,1)}, u32[]{:S(2)}) copy-start(bf16[1,256,512]{2,1,0:T(8,128)(2,1)} %param.7) | copy-start | bytes 786436
  1.3 13.0 %copy-start.5 = (s32[32,1]{0,1:T(1,128)S(1)}, s32[32,1]{0,1:T(1,128)}, u32[]{:S(2)}) copy-start(s32[32,1]{0,1:T(1,128)} %param.11) | copy-start | bytes 388
  1.3 43.7 %copy-start.3 = (s32[32]{0:T(128)S(1)}, s32[32]{0:T(128)}, u32[]{:S(2)}) copy-start(s32[32]{0:T(128)} %structure_ref.14) | copy-start | bytes 388
  4.4 40.0 %collective-permute-start.2 = (bf16[16,2,256,256]{3,2,1,0:T(8,128)(2,1)S(1)}, bf16[16,2,256,256]{3,2,1,0:T(8,128)(2,1)S(1)}, u32[]{:S(2)}, u32[]{:S(2)}) collective-permute-start(bf16[16,2,256,256]{3,2,1,0:T(8,128)(2,1)S(1)} %get-tuple-element.13), channel_id=1, source_target_pairs={{0,1},{1,0},{2,3},{3,2},{4,5},{5,4},{6,7},{7,6},{8,9},{9,8},{10,11... | collective-permute-start | bytes 12582920 | tf_op jit(solution)/shard_map/ppermute | solution.py:63
  7.7 9.4 %collective-permute-start.5 = (bf16[256,512]{1,0:T(8,128)(2,1)S(1)}, bf16[256,512]{1,0:T(8,128)(2,1)S(1)}, u32[]{:S(2)}, u32[]{:S(2)}) collective-permute-start(bf16[256,512]{1,0:T(8,128)(2,1)S(1)} %bitcast.23), channel_id=1, source_target_pairs={{0,2},{1,15},{2,4},{3,1},{4,6},{5,3},{6,8},{7,5},{8,10},{9,7},{10,... | collective-permute-start | bytes 786440 | tf_op jit(solution)/shard_map/ppermute | solution.py:63
  11.6 8.9 %collective-permute-start.3 = (bf16[256,512]{1,0:T(8,128)(2,1)S(1)}, bf16[256,512]{1,0:T(8,128)(2,1)S(1)}, u32[]{:S(2)}, u32[]{:S(2)}) collective-permute-start(bf16[256,512]{1,0:T(8,128)(2,1)S(1)} %bitcast.24), channel_id=1, source_target_pairs={{0,14},{1,3},{2,0},{3,5},{4,2},{5,7},{6,4},{7,9},{8,6},{9,11},{10,... | collective-permute-start | bytes 786440 | tf_op jit(solution)/shard_map/ppermute | solution.py:63
  11.6 8.9 %collective-permute-start.4 = (bf16[256,512]{1,0:T(8,128)(2,1)S(1)}, bf16[256,512]{1,0:T(8,128)(2,1)S(1)}, u32[]{:S(2)}, u32[]{:S(2)}) collective-permute-start(bf16[256,512]{1,0:T(8,128)(2,1)S(1)} %bitcast.25), channel_id=1, source_target_pairs={{0,16},{1,17},{2,18},{3,19},{4,20},{5,21},{6,22},{7,23},{8,24},{9,... | collective-permute-start | bytes 786440 | tf_op jit(solution)/shard_map/ppermute | solution.py:63
  14.5 6.1 %collective-permute-start = (s32[32]{0:T(128)S(1)}, s32[32]{0:T(128)S(1)}, u32[]{:S(2)}, u32[]{:S(2)}) collective-permute-start(s32[32]{0:T(128)S(1)} %multiply_add_fusion), channel_id=1, source_target_pairs={{0,1},{1,0},{2,3},{3,2},{4,5},{5,4},{6,7},{7,6},{8,9},{9,8},{10,11... | collective-permute-start | bytes 392 | tf_op jit(solution)/shard_map/ppermute | solution.py:63
  17.1 10.6 %collective-permute-start.6 = (bf16[256,512]{1,0:T(8,128)(2,1)S(1)}, bf16[256,512]{1,0:T(8,128)(2,1)S(1)}, u32[]{:S(2)}, u32[]{:S(2)}) collective-permute-start(bf16[256,512]{1,0:T(8,128)(2,1)S(1)} %collective-permute-done.5.refs_3_), channel_id=1, source_target_pairs={{0,2},{1,15},{2,4},{3,1},{4,6},{5,3},{6,8},{7,5},{8,10},{9,7},{10,... | collective-permute-start | bytes 786440 | tf_op jit(solution)/shard_map/ppermute | solution.py:63
  20.5 10.5 %collective-permute-start.7 = (bf16[256,512]{1,0:T(8,128)(2,1)S(1)}, bf16[256,512]{1,0:T(8,128)(2,1)S(1)}, u32[]{:S(2)}, u32[]{:S(2)}) collective-permute-start(bf16[256,512]{1,0:T(8,128)(2,1)S(1)} %collective-permute-done.3.refs_1_), channel_id=1, source_target_pairs={{0,14},{1,3},{2,0},{3,5},{4,2},{5,7},{6,4},{7,9},{8,6},{9,11},{10,... | collective-permute-start | bytes 786440 | tf_op jit(solution)/shard_map/ppermute | solution.py:63
  20.5 10.8 %collective-permute-start.8 = (bf16[256,512]{1,0:T(8,128)(2,1)S(1)}, bf16[256,512]{1,0:T(8,128)(2,1)S(1)}, u32[]{:S(2)}, u32[]{:S(2)}) collective-permute-start(bf16[256,512]{1,0:T(8,128)(2,1)S(1)} %collective-permute-done.4.refs_2_), channel_id=1, source_target_pairs={{0,14},{1,3},{2,0},{3,5},{4,2},{5,7},{6,4},{7,9},{8,6},{9,11},{10,... | collective-permute-start | bytes 786440 | tf_op jit(solution)/shard_map/ppermute | solution.py:63
  20.6 4.0 %collective-permute-start.1 = (s32[2,32]{1,0:T(2,128)S(1)}, s32[2,32]{1,0:T(2,128)S(1)}, u32[]{:S(2)}, u32[]{:S(2)}) collective-permute-start(s32[2,32]{1,0:T(2,128)S(1)} %pad_add_fusion.near_ref), channel_id=1, source_target_pairs={{0,16},{1,17},{2,18},{3,19},{4,20},{5,21},{6,22},{7,23},{8,24},{9,... | collective-permute-start | bytes 776 | tf_op jit(solution)/shard_map/ppermute | solution.py:63
  24.6 6.8 %collective-permute-start.9 = (bf16[256,512]{1,0:T(8,128)(2,1)S(1)}, bf16[256,512]{1,0:T(8,128)(2,1)S(1)}, u32[]{:S(2)}, u32[]{:S(2)}) collective-permute-start(bf16[256,512]{1,0:T(8,128)(2,1)S(1)} %collective-permute-done.5.refs_3_), channel_id=1, source_target_pairs={{0,16},{1,17},{2,18},{3,19},{4,20},{5,21},{6,22},{7,23},{8,24},{9,... | collective-permute-start | bytes 786440 | tf_op jit(solution)/shard_map/ppermute | solution.py:63
  27.7 6.6 %collective-permute-start.10 = (bf16[256,512]{1,0:T(8,128)(2,1)S(1)}, bf16[256,512]{1,0:T(8,128)(2,1)S(1)}, u32[]{:S(2)}, u32[]{:S(2)}) collective-permute-start(bf16[256,512]{1,0:T(8,128)(2,1)S(1)} %collective-permute-done.6.refs_1_), channel_id=1, source_target_pairs={{0,2},{1,15},{2,4},{3,1},{4,6},{5,3},{6,8},{7,5},{8,10},{9,7},{10,... | collective-permute-start | bytes 786440 | tf_op jit(solution)/shard_map/ppermute | solution.py:63
  31.0 9.8 %collective-permute-start.13 = (bf16[256,512]{1,0:T(8,128)(2,1)S(1)}, bf16[256,512]{1,0:T(8,128)(2,1)S(1)}, u32[]{:S(2)}, u32[]{:S(2)}) collective-permute-start(bf16[256,512]{1,0:T(8,128)(2,1)S(1)} %collective-permute-done.6.refs_1_), channel_id=1, source_target_pairs={{0,16},{1,17},{2,18},{3,19},{4,20},{5,21},{6,22},{7,23},{8,24},{9,... | collective-permute-start | bytes 786440 | tf_op jit(solution)/shard_map/ppermute | solution.py:63
  31.3 9.6 %collective-permute-start.12 = (bf16[256,512]{1,0:T(8,128)(2,1)S(1)}, bf16[256,512]{1,0:T(8,128)(2,1)S(1)}, u32[]{:S(2)}, u32[]{:S(2)}) collective-permute-start(bf16[256,512]{1,0:T(8,128)(2,1)S(1)} %collective-permute-done.8.refs_3_), channel_id=1, source_target_pairs={{0,14},{1,3},{2,0},{3,5},{4,2},{5,7},{6,4},{7,9},{8,6},{9,11},{10,... | collective-permute-start | bytes 786440 | tf_op jit(solution)/shard_map/ppermute | solution.py:63
  31.5 17.3 %collective-permute-start.11 = (bf16[256,512]{1,0:T(8,128)(2,1)S(1)}, bf16[256,512]{1,0:T(8,128)(2,1)S(1)}, u32[]{:S(2)}, u32[]{:S(2)}) collective-permute-start(bf16[256,512]{1,0:T(8,128)(2,1)S(1)} %collective-permute-done.7.refs_2_), channel_id=1, source_target_pairs={{0,14},{1,3},{2,0},{3,5},{4,2},{5,7},{6,4},{7,9},{8,6},{9,11},{10,... | collective-permute-start | bytes 786440 | tf_op jit(solution)/shard_map/ppermute | solution.py:63
  34.3 16.6 %collective-permute-start.14 = (bf16[256,512]{1,0:T(8,128)(2,1)S(1)}, bf16[256,512]{1,0:T(8,128)(2,1)S(1)}, u32[]{:S(2)}, u32[]{:S(2)}) collective-permute-start(bf16[256,512]{1,0:T(8,128)(2,1)S(1)} %collective-permute-done.10.refs_1_), channel_id=1, source_target_pairs={{0,2},{1,15},{2,4},{3,1},{4,6},{5,3},{6,8},{7,5},{8,10},{9,7},{10,... | collective-permute-start | bytes 786440 | tf_op jit(solution)/shard_map/ppermute | solution.py:63
  40.8 10.9 %collective-permute-start.16 = (bf16[256,512]{1,0:T(8,128)(2,1)S(1)}, bf16[256,512]{1,0:T(8,128)(2,1)S(1)}, u32[]{:S(2)}, u32[]{:S(2)}) collective-permute-start(bf16[256,512]{1,0:T(8,128)(2,1)S(1)} %collective-permute-done.10.refs_1_), channel_id=1, source_target_pairs={{0,16},{1,17},{2,18},{3,19},{4,20},{5,21},{6,22},{7,23},{8,24},{9,... | collective-permute-start | bytes 786440 | tf_op jit(solution)/shard_map/ppermute | solution.py:63
  40.8 10.9 %collective-permute-start.17 = (bf16[256,512]{1,0:T(8,128)(2,1)S(1)}, bf16[256,512]{1,0:T(8,128)(2,1)S(1)}, u32[]{:S(2)}, u32[]{:S(2)}) collective-permute-start(bf16[256,512]{1,0:T(8,128)(2,1)S(1)} %collective-permute-done.10.refs_1_), channel_id=1, source_target_pairs={{0,18},{1,31},{2,20},{3,17},{4,22},{5,19},{6,24},{7,21},{8,26},{9,... | collective-permute-start | bytes 786440 | tf_op jit(solution)/shard_map/ppermute | solution.py:63
  44.5 9.5 %collective-permute-start.15 = (bf16[256,512]{1,0:T(8,128)(2,1)S(1)}, bf16[256,512]{1,0:T(8,128)(2,1)S(1)}, u32[]{:S(2)}, u32[]{:S(2)}) collective-permute-start(bf16[256,512]{1,0:T(8,128)(2,1)S(1)} %collective-permute-done.12.refs_3_), channel_id=1, source_target_pairs={{0,14},{1,3},{2,0},{3,5},{4,2},{5,7},{6,4},{7,9},{8,6},{9,11},{10,... | collective-permute-start | bytes 786440 | tf_op jit(solution)/shard_map/ppermute | solution.py:63
  48.7 5.3 %copy-start.4 = (f32[1,2]{1,0:T(1,128)S(1)}, f32[1,2]{1,0:T(1,128)}, u32[]{:S(2)}) copy-start(f32[1,2]{1,0:T(1,128)} %weight_ref.3) | copy-start | bytes 28
  50.9 9.1 %copy-start.1 = (bf16[1,256,512]{2,1,0:T(8,128)(2,1)S(1)}, bf16[1,256,512]{2,1,0:T(8,128)(2,1)}, u32[]{:S(2)}) copy-start(bf16[1,256,512]{2,1,0:T(8,128)(2,1)} %diag_ref.1) | copy-start | bytes 786436
  55.8 4.3 %collective-permute-start.18 = (f32[2,256,256]{2,1,0:T(8,128)S(1)}, f32[2,256,256]{2,1,0:T(8,128)S(1)}, u32[]{:S(2)}, u32[]{:S(2)}) collective-permute-start(f32[2,256,256]{2,1,0:T(8,128)S(1)} %get-tuple-element.15), channel_id=1, source_target_pairs={{0,1},{1,0},{2,3},{3,2},{4,5},{5,4},{6,7},{7,6},{8,9},{9,8},{10,11... | collective-permute-start | bytes 1572872 | tf_op jit(solution)/shard_map/ppermute | solution.py:63
  (1 other events, 0.7 us)
